TPU v7x, 32 devices: a whole 2x2x4 slice. The times are simulated.
32 devices in a mesh: seq: 16 (over z, x, core), dp: 2 (over y).
Axes of the slice: x: 2, y: 2, z: 4, core: 2. Of those that a mesh axis runs over, the one named last changes fastest.
Arguments:
- queries: bfloat16 [2, 1024, 2048], P(None, 'seq', 'dp'), may hold values from -10 to 10
- key_rows: bfloat16 [2, 1024, 2048], P(None, 'seq', 'dp'), may hold values from -10 to 10
- value_rows: bfloat16 [2, 1024, 2048], P(None, 'seq', 'dp'), may hold values from -6 to 6
- query_tangent: bfloat16 [2, 1024, 2048], P(None, 'seq', 'dp'), may hold values from -6 to 6
- key_tangent: bfloat16 [2, 1024, 2048], P(None, 'seq', 'dp'), may hold values from -6 to 6
- out_adjoint: bfloat16 [2, 1024, 2048], P(None, 'seq', 'dp'), may hold values from -6 to 6
Outputs:
- query_product: bfloat16 [2, 1024, 2048], P(None, 'seq', 'dp')
- key_product: bfloat16 [2, 1024, 2048], P(None, 'seq', 'dp')
- value_product: bfloat16 [2, 1024, 2048], P(None, 'seq', 'dp')
- curvature: float32 [2, 16], replicated
All inputs are finite; a program needn't handle non-finite values.
Results may differ from a plain program's by a relative error of at most 0.0051.
Values may be sent and summed in bfloat16 or wider, within the bound.
A program may use at most 64 MiB of HBM per device.

v0:
```python
import jax
import jax.numpy as jnp
from jax import lax
from jax.sharding import PartitionSpec as P

HEAD_DIM = 128


def inner_rows(left, right):
    return lax.dot_general(
        left, right, (((1,), (1,)), ((), ())), preferred_element_type=jnp.float32
    )


def inner_cols(left, right):
    return lax.dot_general(
        left, right, (((0,), (0,)), ((), ())), preferred_element_type=jnp.float32
    )


def score_block(query, keyset, tquery, tkey, start, block_size):
    factor = HEAD_DIM ** (-0.5)
    stop = start + block_size
    query_block = query[start:stop]
    key_block = keyset[:stop]
    scores = factor * inner_rows(query_block, key_block)
    row_index = start + jnp.arange(block_size)[:, None]
    col_index = jnp.arange(stop)[None, :]
    scores = jnp.where(row_index >= col_index, scores, -jnp.inf)
    top_score = jnp.max(scores, axis=1, keepdims=True)
    weights = jnp.exp(scores - top_score)
    probs = weights / jnp.sum(weights, axis=1, keepdims=True)
    tangent_scores = factor * (
        inner_rows(tquery[start:stop], key_block) + inner_rows(query_block, tkey[:stop])
    )
    mean_tangent = jnp.sum(probs * tangent_scores, axis=1, keepdims=True)
    tangent_probs = probs * (tangent_scores - mean_tangent)
    return (probs, tangent_probs)


def head_work(tensors):
    query, keyset, values_in, tquery, tkey, adjoint = tensors
    factor = HEAD_DIM ** (-0.5)
    length = query.shape[0]
    block_size = min(512, length)
    key_hvp = jnp.zeros((length, HEAD_DIM), jnp.float32)
    value_hvp = jnp.zeros((length, HEAD_DIM), jnp.float32)
    query_parts = []
    for number in range(length // block_size):
        start = number * block_size
        stop = start + block_size
        probs, tangent_probs = score_block(query, keyset, tquery, tkey, start, block_size)
        adj_block = adjoint[start:stop]
        grad_probs = inner_rows(adj_block, values_in[:stop])
        delta = jnp.sum(probs * grad_probs, axis=1, keepdims=True)
        centered = grad_probs - delta
        grad_scores = probs * centered
        tangent_delta = jnp.sum(tangent_probs * grad_probs, axis=1, keepdims=True)
        second_scores = tangent_probs * centered - probs * tangent_delta
        tprob_low = tangent_probs.astype(jnp.bfloat16)
        gscore_low = grad_scores.astype(jnp.bfloat16)
        second_low = second_scores.astype(jnp.bfloat16)
        value_hvp = value_hvp.at[:stop].add(inner_cols(tprob_low, adj_block))
        query_parts.append(
            factor
            * (
                jnp.dot(second_low, keyset[:stop], preferred_element_type=jnp.float32)
                + jnp.dot(gscore_low, tkey[:stop], preferred_element_type=jnp.float32)
            )
        )
        key_hvp = key_hvp.at[:stop].add(
            factor
            * (
                inner_cols(second_low, query[start:stop])
                + inner_cols(gscore_low, tquery[start:stop])
            )
        )
    query_hvp = jnp.concatenate(query_parts, axis=0)
    kappa = jnp.sum(tquery.astype(jnp.float32) * query_hvp) + jnp.sum(
        tkey.astype(jnp.float32) * key_hvp
    )
    return (query_hvp, key_hvp, value_hvp, kappa)


def local(queries, key_rows, value_rows, query_tangent, key_tangent, out_adjoint):
    batch_count = queries.shape[0]
    tokens_here = queries.shape[1]
    local_heads = queries.shape[2] // HEAD_DIM

    def to_items(tensor):
        shaped = tensor.reshape(batch_count, tokens_here, local_heads, HEAD_DIM)
        return jnp.transpose(shaped, (0, 2, 1, 3)).reshape(
            batch_count * local_heads, tokens_here, HEAD_DIM
        )

    parts = (
        lax.all_to_all(to_items(queries), "seq", split_axis=0, concat_axis=1, tiled=True),
        lax.all_to_all(to_items(key_rows), "seq", split_axis=0, concat_axis=1, tiled=True),
        lax.all_to_all(to_items(value_rows), "seq", split_axis=0, concat_axis=1, tiled=True),
        lax.all_to_all(to_items(query_tangent), "seq", split_axis=0, concat_axis=1, tiled=True),
        lax.all_to_all(to_items(key_tangent), "seq", split_axis=0, concat_axis=1, tiled=True),
        lax.all_to_all(to_items(out_adjoint), "seq", split_axis=0, concat_axis=1, tiled=True),
    )
    item_count = parts[0].shape[0]
    item = 0
    tensors = tuple((part[item] for part in parts))
    query_hvp, key_hvp, value_hvp, kappa = head_work(tensors)
    query_items = [query_hvp.astype(jnp.bfloat16)]
    key_items = [key_hvp.astype(jnp.bfloat16)]
    value_items = [value_hvp.astype(jnp.bfloat16)]
    kappas = [kappa]
    returned = (
        lax.all_to_all(jnp.stack(query_items), "seq", split_axis=1, concat_axis=0, tiled=True),
        lax.all_to_all(jnp.stack(key_items), "seq", split_axis=1, concat_axis=0, tiled=True),
        lax.all_to_all(jnp.stack(value_items), "seq", split_axis=1, concat_axis=0, tiled=True),
    )

    def to_tokens(tensor):
        shaped = tensor.reshape(batch_count, local_heads, tokens_here, HEAD_DIM)
        return jnp.transpose(shaped, (0, 2, 1, 3)).reshape(
            batch_count, tokens_here, local_heads * HEAD_DIM
        )

    outputs = tuple((to_tokens(piece) for piece in returned))
    heads_total = local_heads * lax.axis_size("dp")
    batch_index = jnp.arange(batch_count)[:, None]
    head_index = jnp.arange(heads_total)[None, :]
    item = 0
    global_item = lax.axis_index("seq") * item_count + item
    batch_here = global_item // local_heads
    head_here = lax.axis_index("dp") * local_heads + global_item % local_heads
    hit = jnp.logical_and(batch_index == batch_here, head_index == head_here)
    board = jnp.where(hit, kappas[item], 0.0)
    curvature = lax.psum(board, ("seq", "dp"))
    return (outputs[0], outputs[1], outputs[2], curvature)


def solution(mesh):
    return jax.shard_map(
        local,
        mesh=mesh,
        in_specs=(
            P(None, "seq", "dp"),
            P(None, "seq", "dp"),
            P(None, "seq", "dp"),
            P(None, "seq", "dp"),
            P(None, "seq", "dp"),
            P(None, "seq", "dp"),
        ),
        out_specs=(P(None, "seq", "dp"), P(None, "seq", "dp"), P(None, "seq", "dp"), P()),
        check_vma=False,
    )
```

profile of v0, /device:TPU:0, one launch (start us, length us, event | category | flops | bytes accessed | tf_op | source)
XLA Modules:
  0.0 181.6 jit_solution(2033972565623164572)
XLA Ops:
  2.5 7.4 %all-to-all-start = ((bf16[16,64,128]{2,1,0:T(8,128)(2,1)}), bf16[16,64,128]{2,1,0:T(8,128)(2,1)S(1)}, u32[]{:S(2)}, u32[]{:S(2)}) async-start(bf16[16,64,128]{2,1,0:T(8,128)(2,1)} %bitcast.1), calls=%async_computation | async-start | bytes 524288 | tf_op jit(solution)/shard_map/all_to_all | solution.py:97
  10.9 9.0 %all-to-all-done = bf16[16,64,128]{2,1,0:T(8,128)(2,1)S(1)} async-done(((bf16[16,64,128]{2,1,0:T(8,128)(2,1)}), bf16[16,64,128]{2,1,0:T(8,128)(2,1)S(1)}, u32[]{:S(2)}, u32[]{:S(2)}) %all-to-all-start) | async-done | bytes 262176 | tf_op jit(solution)/shard_map/all_to_all | solution.py:97
  19.9 3.5 %all-to-all-start.1 = ((bf16[16,64,128]{2,1,0:T(8,128)(2,1)}), bf16[16,64,128]{2,1,0:T(8,128)(2,1)S(1)}, u32[]{:S(2)}, u32[]{:S(2)}) async-start(bf16[16,64,128]{2,1,0:T(8,128)(2,1)} %bitcast.4), calls=%async_computation.1 | async-start | bytes 524288 | tf_op jit(solution)/shard_map/all_to_all | solution.py:98
  24.4 9.0 %all-to-all-done.1 = bf16[16,64,128]{2,1,0:T(8,128)(2,1)S(1)} async-done(((bf16[16,64,128]{2,1,0:T(8,128)(2,1)}), bf16[16,64,128]{2,1,0:T(8,128)(2,1)S(1)}, u32[]{:S(2)}, u32[]{:S(2)}) %all-to-all-start.1) | async-done | bytes 262176 | tf_op jit(solution)/shard_map/all_to_all | solution.py:98
  33.4 3.5 %all-to-all-start.2 = ((bf16[16,64,128]{2,1,0:T(8,128)(2,1)}), bf16[16,64,128]{2,1,0:T(8,128)(2,1)S(1)}, u32[]{:S(2)}, u32[]{:S(2)}) async-start(bf16[16,64,128]{2,1,0:T(8,128)(2,1)} %bitcast.7), calls=%async_computation.2 | async-start | bytes 524288 | tf_op jit(solution)/shard_map/all_to_all | solution.py:100
  40.5 6.5 %all-to-all-done.2 = bf16[16,64,128]{2,1,0:T(8,128)(2,1)S(1)} async-done(((bf16[16,64,128]{2,1,0:T(8,128)(2,1)}), bf16[16,64,128]{2,1,0:T(8,128)(2,1)S(1)}, u32[]{:S(2)}, u32[]{:S(2)}) %all-to-all-start.2) | async-done | bytes 262176 | tf_op jit(solution)/shard_map/all_to_all | solution.py:100
  47.0 3.5 %all-to-all-start.4 = ((bf16[16,64,128]{2,1,0:T(8,128)(2,1)}), bf16[16,64,128]{2,1,0:T(8,128)(2,1)S(1)}, u32[]{:S(2)}, u32[]{:S(2)}) async-start(bf16[16,64,128]{2,1,0:T(8,128)(2,1)} %bitcast.13), calls=%async_computation.4 | async-start | bytes 524288 | tf_op jit(solution)/shard_map/all_to_all | solution.py:102
  51.8 1.8 fusion.25
  53.6 6.9 %all-to-all-done.4 = bf16[16,64,128]{2,1,0:T(8,128)(2,1)S(1)} async-done(((bf16[16,64,128]{2,1,0:T(8,128)(2,1)}), bf16[16,64,128]{2,1,0:T(8,128)(2,1)S(1)}, u32[]{:S(2)}, u32[]{:S(2)}) %all-to-all-start.4) | async-done | bytes 262176 | tf_op jit(solution)/shard_map/all_to_all | solution.py:102
  60.5 3.5 %all-to-all-start.3 = ((bf16[16,64,128]{2,1,0:T(8,128)(2,1)}), bf16[16,64,128]{2,1,0:T(8,128)(2,1)S(1)}, u32[]{:S(2)}, u32[]{:S(2)}) async-start(bf16[16,64,128]{2,1,0:T(8,128)(2,1)} %bitcast.10), calls=%async_computation.3 | async-start | bytes 524288 | tf_op jit(solution)/shard_map/all_to_all | solution.py:101
  65.3 8.7 %all-to-all-done.3 = bf16[16,64,128]{2,1,0:T(8,128)(2,1)S(1)} async-done(((bf16[16,64,128]{2,1,0:T(8,128)(2,1)}), bf16[16,64,128]{2,1,0:T(8,128)(2,1)S(1)}, u32[]{:S(2)}, u32[]{:S(2)}) %all-to-all-start.3) | async-done | bytes 262176 | tf_op jit(solution)/shard_map/all_to_all | solution.py:101
  74.0 3.7 %all-to-all-start.5 = ((bf16[16,64,128]{2,1,0:T(8,128)(2,1)}), bf16[16,64,128]{2,1,0:T(8,128)(2,1)S(1)}, u32[]{:S(2)}, u32[]{:S(2)}) async-start(bf16[16,64,128]{2,1,0:T(8,128)(2,1)} %bitcast.16), calls=%async_computation.5 | async-start | bytes 524288 | tf_op jit(solution)/shard_map/all_to_all | solution.py:99
  79.3 2.1 %multiply_reduce_fusion.2 = (f32[512]{0:T(512)S(1)}, f32[512,1024]{1,0:T(8,128)}) fusion(f32[512]{0:T(512)S(1)} %fusion.1, f32[512,1024]{1,0:T(8,128)S(1)} %get-tuple-element.85, f32[512]{0:T(512)S(1)} %get-tuple-element.84, f32[512,1024]{1,0:T(8,128)S(1)} %copy-done.8, bf16[512,128]{1,0:T(8,128)(2,1)S(1)} %bitcast.176, bf16[1024,128]{1,0:T(8,128)(2,1)S(1)} %bitcast.144), kind=kOutput, calls=%fused_computation.5 | convolution fusion | flops 137362944 | bytes 6690816 | tf_op jit(solution)/shard_map/dot_general | solution.py:10
  81.4 6.1 %all-to-all-done.5 = bf16[16,64,128]{2,1,0:T(8,128)(2,1)S(1)} async-done(((bf16[16,64,128]{2,1,0:T(8,128)(2,1)}), bf16[16,64,128]{2,1,0:T(8,128)(2,1)S(1)}, u32[]{:S(2)}, u32[]{:S(2)}) %all-to-all-start.5) | async-done | bytes 262176 | tf_op jit(solution)/shard_map/all_to_all | solution.py:99
  87.5 2.7 %multiply_reduce_fusion.1 = (f32[512]{0:T(512)S(1)}, f32[512]{0:T(512)S(1)}, f32[512,1024]{1,0:T(8,128)S(1)}) fusion(f32[512]{0:T(512)S(1)} %fusion.1, f32[512,1024]{1,0:T(8,128)S(1)} %get-tuple-element.85, f32[512]{0:T(512)S(1)} %get-tuple-element.84, f32[512,1024]{1,0:T(8,128)} %get-tuple-element.87, f32[512]{0:T(512)S(1)} %get-tuple-element.86, ...), kind=kOutput, calls=%fused_computation.3 | convolution fusion | flops 138411008 | bytes 6694912 | tf_op jit(solution)/shard_map/dot_general | solution.py:10
  90.3 1.2 multiply_convert_fusion
  91.6 1.1 fusion.26
  92.7 1.3 fusion.28
  97.3 1.3 multiply_convert_fusion.1
  99.7 1.2 fusion.9
  101.8 2.2 %reduce.12 = bf16[1024,128]{1,0:T(8,128)(2,1)S(1)} reduce(bf16[1024,1,128]{2,1,0:T(2,128)(2,1)S(1)} %bitcast.149, bf16[]{:T(256)} %broadcast.116), dimensions={1}, to_apply=%bitcast.132.reduce_sub_computation | reduce | bytes 524290
  104.8 3.8 %all-to-all-start.8 = ((bf16[16,2,4096]{2,1,0:T(2,128)(2,1)}), bf16[16,2,4096]{2,1,0:T(2,128)(2,1)S(1)}, u32[]{:S(2)}, u32[]{:S(2)}) async-start(bf16[16,2,4096]{2,1,0:T(2,128)(2,1)} %reshape.297), calls=%async_computation.8 | async-start | bytes 524288 | tf_op jit(solution)/shard_map/all_to_all | solution.py:115
  108.6 1.2 fusion.8
  109.9 1.2 multiply_reduce_fusion.6
  111.5 2.9 %reduce.13 = bf16[1024,128]{1,0:T(8,128)(2,1)} reduce(bf16[1024,1,128]{2,1,0:T(2,128)(2,1)S(1)} %bitcast.152, bf16[]{:T(256)} %broadcast.116), dimensions={1}, to_apply=%bitcast.133.reduce_sub_computation | reduce | bytes 524290
  114.4 1.7 reshape.295
  116.9 1.4 all-to-all-done.8
  118.4 4.3 %all-to-all-start.7 = ((bf16[16,2,4096]{2,1,0:T(2,128)(2,1)}), bf16[16,2,4096]{2,1,0:T(2,128)(2,1)S(1)}, u32[]{:S(2)}, u32[]{:S(2)}) async-start(bf16[16,2,4096]{2,1,0:T(2,128)(2,1)} %reshape.295), calls=%async_computation.7 | async-start | bytes 524288 | tf_op jit(solution)/shard_map/all_to_all | solution.py:114
  123.6 2.2 %reduce.11 = bf16[1024,128]{1,0:T(8,128)(2,1)S(1)} reduce(bf16[1024,1,128]{2,1,0:T(2,128)(2,1)S(1)} %bitcast.151, bf16[]{:T(256)} %broadcast.116), dimensions={1}, to_apply=%bitcast.134.reduce_sub_computation | reduce | bytes 524290
  126.5 6.2 %all-to-all-done.7 = bf16[16,2,4096]{2,1,0:T(2,128)(2,1)S(1)} async-done(((bf16[16,2,4096]{2,1,0:T(2,128)(2,1)}), bf16[16,2,4096]{2,1,0:T(2,128)(2,1)S(1)}, u32[]{:S(2)}, u32[]{:S(2)}) %all-to-all-start.7) | async-done | bytes 262176 | tf_op jit(solution)/shard_map/all_to_all | solution.py:114
  132.7 3.5 %all-to-all-start.6 = ((bf16[16,2,4096]{2,1,0:T(2,128)(2,1)}), bf16[16,2,4096]{2,1,0:T(2,128)(2,1)S(1)}, u32[]{:S(2)}, u32[]{:S(2)}) async-start(bf16[16,2,4096]{2,1,0:T(2,128)(2,1)} %reshape.293), calls=%async_computation.6 | async-start | bytes 524288 | tf_op jit(solution)/shard_map/all_to_all | solution.py:113
  138.5 40.5 %psum.7 = f32[2,16]{1,0:T(2,128)} all-reduce(f32[2,16]{1,0:T(2,128)S(1)} %and_select_fusion), channel_id=1, replica_groups=mesh['seq'=16,'dp'=2] {'seq','dp'}, use_global_device_ids=true, to_apply=%region_12.13 | all-reduce | flops 32 | bytes 256 | tf_op jit(solution)/shard_map/psum | solution.py:134
  (119 shorter events, 23.6 us)
Async XLA Ops:
  0.6 9.3 %copy-start.21 = (bf16[2,64,1024]{2,1,0:T(8,128)(2,1)S(1)}, bf16[2,64,1024]{2,1,0:T(8,128)(2,1)}, u32[]{:S(2)}) copy-start(bf16[2,64,1024]{2,1,0:T(8,128)(2,1)} %param.19) | copy-start | bytes 786436
  0.6 10.1 %copy-start.22 = (bf16[2,64,1024]{2,1,0:T(8,128)(2,1)S(1)}, bf16[2,64,1024]{2,1,0:T(8,128)(2,1)}, u32[]{:S(2)}) copy-start(bf16[2,64,1024]{2,1,0:T(8,128)(2,1)} %param.20) | copy-start | bytes 786436
  0.7 10.2 %copy-start.23 = (bf16[2,64,1024]{2,1,0:T(8,128)(2,1)S(1)}, bf16[2,64,1024]{2,1,0:T(8,128)(2,1)}, u32[]{:S(2)}) copy-start(bf16[2,64,1024]{2,1,0:T(8,128)(2,1)} %param.21) | copy-start | bytes 786436
  2.5 17.4 %all-to-all-start = ((bf16[16,64,128]{2,1,0:T(8,128)(2,1)}), bf16[16,64,128]{2,1,0:T(8,128)(2,1)S(1)}, u32[]{:S(2)}, u32[]{:S(2)}) async-start(bf16[16,64,128]{2,1,0:T(8,128)(2,1)} %bitcast.1), calls=%async_computation | async-start | bytes 524288 | tf_op jit(solution)/shard_map/all_to_all | solution.py:97
  10.0 14.3 %copy-start.24 = (bf16[2,64,1024]{2,1,0:T(8,128)(2,1)S(1)}, bf16[2,64,1024]{2,1,0:T(8,128)(2,1)}, u32[]{:S(2)}) copy-start(bf16[2,64,1024]{2,1,0:T(8,128)(2,1)} %param.22) | copy-start | bytes 786436
  10.0 14.3 %copy-start.25 = (bf16[2,64,1024]{2,1,0:T(8,128)(2,1)S(1)}, bf16[2,64,1024]{2,1,0:T(8,128)(2,1)}, u32[]{:S(2)}) copy-start(bf16[2,64,1024]{2,1,0:T(8,128)(2,1)} %param.23) | copy-start | bytes 786436
  19.9 13.5 %all-to-all-start.1 = ((bf16[16,64,128]{2,1,0:T(8,128)(2,1)}), bf16[16,64,128]{2,1,0:T(8,128)(2,1)S(1)}, u32[]{:S(2)}, u32[]{:S(2)}) async-start(bf16[16,64,128]{2,1,0:T(8,128)(2,1)} %bitcast.4), calls=%async_computation.1 | async-start | bytes 524288 | tf_op jit(solution)/shard_map/all_to_all | solution.py:98
  33.4 13.5 %all-to-all-start.2 = ((bf16[16,64,128]{2,1,0:T(8,128)(2,1)}), bf16[16,64,128]{2,1,0:T(8,128)(2,1)S(1)}, u32[]{:S(2)}, u32[]{:S(2)}) async-start(bf16[16,64,128]{2,1,0:T(8,128)(2,1)} %bitcast.7), calls=%async_computation.2 | async-start | bytes 524288 | tf_op jit(solution)/shard_map/all_to_all | solution.py:100
  47.0 13.5 %copy-start.6 = (bf16[16,64,128]{2,1,0:T(8,128)(2,1)}, bf16[16,64,128]{2,1,0:T(8,128)(2,1)S(1)}, u32[]{:S(2)}) copy-start(bf16[16,64,128]{2,1,0:T(8,128)(2,1)S(1)} %all-to-all-done.2) | copy-start | bytes 786436
  47.0 13.5 %all-to-all-start.4 = ((bf16[16,64,128]{2,1,0:T(8,128)(2,1)}), bf16[16,64,128]{2,1,0:T(8,128)(2,1)S(1)}, u32[]{:S(2)}, u32[]{:S(2)}) async-start(bf16[16,64,128]{2,1,0:T(8,128)(2,1)} %bitcast.13), calls=%async_computation.4 | async-start | bytes 524288 | tf_op jit(solution)/shard_map/all_to_all | solution.py:102
  60.5 13.5 %all-to-all-start.3 = ((bf16[16,64,128]{2,1,0:T(8,128)(2,1)}), bf16[16,64,128]{2,1,0:T(8,128)(2,1)S(1)}, u32[]{:S(2)}, u32[]{:S(2)}) async-start(bf16[16,64,128]{2,1,0:T(8,128)(2,1)} %bitcast.10), calls=%async_computation.3 | async-start | bytes 524288 | tf_op jit(solution)/shard_map/all_to_all | solution.py:101
  64.7 22.8 %copy-start.26 = (bf16[8,64,128]{2,1,0:T(8,128)(2,1)}, bf16[8,64,128]{2,1,0:T(8,128)(2,1)S(1)}, u32[]{:S(2)}) copy-start(bf16[8,64,128]{2,1,0:T(8,128)(2,1)S(1)} %get-tuple-element.83) | copy-start | bytes 393220
  74.0 7.4 %copy-start.3 = (bf16[16,64,128]{2,1,0:T(8,128)(2,1)}, bf16[16,64,128]{2,1,0:T(8,128)(2,1)S(1)}, u32[]{:S(2)}) copy-start(bf16[16,64,128]{2,1,0:T(8,128)(2,1)S(1)} %all-to-all-done.3) | copy-start | bytes 786436
  74.0 13.5 %all-to-all-start.5 = ((bf16[16,64,128]{2,1,0:T(8,128)(2,1)}), bf16[16,64,128]{2,1,0:T(8,128)(2,1)S(1)}, u32[]{:S(2)}, u32[]{:S(2)}) async-start(bf16[16,64,128]{2,1,0:T(8,128)(2,1)} %bitcast.16), calls=%async_computation.5 | async-start | bytes 524288 | tf_op jit(solution)/shard_map/all_to_all | solution.py:99
  87.5 2.7 %copy-start.16 = (bf16[16,64,128]{2,1,0:T(8,128)(2,1)}, bf16[16,64,128]{2,1,0:T(8,128)(2,1)S(1)}, u32[]{:S(2)}) copy-start(bf16[16,64,128]{2,1,0:T(8,128)(2,1)S(1)} %all-to-all-done.5) | copy-start | bytes 786436
  87.5 2.7 %copy-start.10 = (f32[512,1024]{1,0:T(8,128)S(1)}, f32[512,1024]{1,0:T(8,128)}, u32[]{:S(2)}) copy-start(f32[512,1024]{1,0:T(8,128)} %get-tuple-element.87) | copy-start | bytes 6291460
  91.5 2.5 %copy-start.11 = (bf16[8,64,128]{2,1,0:T(8,128)(2,1)S(1)}, bf16[8,64,128]{2,1,0:T(8,128)(2,1)}, u32[]{:S(2)}) copy-start(bf16[8,64,128]{2,1,0:T(8,128)(2,1)} %get-tuple-element.78) | copy-start | bytes 393220
  91.5 2.8 %copy-start.20 = (bf16[8,64,128]{2,1,0:T(8,128)(2,1)S(1)}, bf16[8,64,128]{2,1,0:T(8,128)(2,1)}, u32[]{:S(2)}) copy-start(bf16[8,64,128]{2,1,0:T(8,128)(2,1)} %get-tuple-element.80) | copy-start | bytes 393220
  97.3 2.4 %copy-start.27 = (bf16[8,64,128]{2,1,0:T(8,128)(2,1)S(1)}, bf16[8,64,128]{2,1,0:T(8,128)(2,1)}, u32[]{:S(2)}) copy-start(bf16[8,64,128]{2,1,0:T(8,128)(2,1)} %copy-done.26) | copy-start | bytes 393220
  100.9 7.7 %copy-start.2 = (bf16[512,512]{0,1:T(8,128)(2,1)S(1)}, bf16[512,512]{0,1:T(8,128)(2,1)}, u32[]{:S(2)}) copy-start(bf16[512,512]{0,1:T(8,128)(2,1)} %get-tuple-element.74) | copy-start | bytes 1572868
  100.9 7.7 %copy-start.12 = (bf16[8,64,128]{2,1,0:T(8,128)(2,1)S(1)}, bf16[8,64,128]{2,1,0:T(8,128)(2,1)}, u32[]{:S(2)}) copy-start(bf16[8,64,128]{2,1,0:T(8,128)(2,1)} %get-tuple-element.78) | copy-start | bytes 393220
  100.9 9.0 %copy-start.5 = (bf16[16,64,128]{2,1,0:T(8,128)(2,1)S(1)}, bf16[16,64,128]{2,1,0:T(8,128)(2,1)}, u32[]{:S(2)}) copy-start(bf16[16,64,128]{2,1,0:T(8,128)(2,1)} %copy-done.3) | copy-start | bytes 786436
  100.9 9.0 %copy-start.9 = (f32[1024,128]{1,0:T(8,128)S(1)}, f32[1024,128]{1,0:T(8,128)}, u32[]{:S(2)}) copy-start(f32[1024,128]{1,0:T(8,128)} %fusion.28) | copy-start | bytes 1572868
  100.9 9.0 %copy-start.14 = (bf16[8,64,128]{2,1,0:T(8,128)(2,1)S(1)}, bf16[8,64,128]{2,1,0:T(8,128)(2,1)}, u32[]{:S(2)}) copy-start(bf16[8,64,128]{2,1,0:T(8,128)(2,1)} %copy-done.13) | copy-start | bytes 393220
  104.8 13.5 %all-to-all-start.8 = ((bf16[16,2,4096]{2,1,0:T(2,128)(2,1)}), bf16[16,2,4096]{2,1,0:T(2,128)(2,1)S(1)}, u32[]{:S(2)}, u32[]{:S(2)}) async-start(bf16[16,2,4096]{2,1,0:T(2,128)(2,1)} %reshape.297), calls=%async_computation.8 | async-start | bytes 524288 | tf_op jit(solution)/shard_map/all_to_all | solution.py:115
  109.9 6.2 %copy-start.1 = (bf16[512,512]{0,1:T(8,128)(2,1)S(1)}, bf16[512,512]{0,1:T(8,128)(2,1)}, u32[]{:S(2)}) copy-start(bf16[512,512]{0,1:T(8,128)(2,1)} %copy-done) | copy-start | bytes 1572868
  111.1 5.4 %copy-start.15 = (f32[512,128]{1,0:T(8,128)S(1)}, f32[512,128]{1,0:T(8,128)}, u32[]{:S(2)}) copy-start(f32[512,128]{1,0:T(8,128)} %fusion.26) | copy-start | bytes 786436
  116.5 6.2 %copy-start.19 = (bf16[8,64,128]{2,1,0:T(8,128)(2,1)S(1)}, bf16[8,64,128]{2,1,0:T(8,128)(2,1)}, u32[]{:S(2)}) copy-start(bf16[8,64,128]{2,1,0:T(8,128)(2,1)} %copy-done.18) | copy-start | bytes 393220
  118.4 14.3 %all-to-all-start.7 = ((bf16[16,2,4096]{2,1,0:T(2,128)(2,1)}), bf16[16,2,4096]{2,1,0:T(2,128)(2,1)S(1)}, u32[]{:S(2)}, u32[]{:S(2)}) async-start(bf16[16,2,4096]{2,1,0:T(2,128)(2,1)} %reshape.295), calls=%async_computation.7 | async-start | bytes 524288 | tf_op jit(solution)/shard_map/all_to_all | solution.py:114
  123.1 13.2 %copy-start.7 = (bf16[16,64,128]{2,1,0:T(8,128)(2,1)S(1)}, bf16[16,64,128]{2,1,0:T(8,128)(2,1)}, u32[]{:S(2)}) copy-start(bf16[16,64,128]{2,1,0:T(8,128)(2,1)} %copy-done.6) | copy-start | bytes 786436
  123.1 15.3 %copy-start.29 = (pred[16]{0:T(512)(128)(4,1)S(1)}, pred[16]{0:T(512)(128)(4,1)}, u32[]{:S(2)}) copy-start(pred[16]{0:T(512)(128)(4,1)} %iota_compare_fusion.2) | copy-start | bytes 52
  132.7 47.0 %all-to-all-start.6 = ((bf16[16,2,4096]{2,1,0:T(2,128)(2,1)}), bf16[16,2,4096]{2,1,0:T(2,128)(2,1)S(1)}, u32[]{:S(2)}, u32[]{:S(2)}) async-start(bf16[16,2,4096]{2,1,0:T(2,128)(2,1)} %reshape.293), calls=%async_computation.6 | async-start | bytes 524288 | tf_op jit(solution)/shard_map/all_to_all | solution.py:113
  (7 other events, 7.9 us)
where the time goes:
time: 183 us; the launch traced here: 182 us
  waiting for transfers between devices  53.8 us (29%)
  blocking collectives  40.5 us (22%)
  starting transfers between devices  36.8 us (20%)
  local copies, waits for them, and re-layouts  18.6 us (10%)
  matrix products  17.2 us (9%)
  other arithmetic  12 us (7%)
  between operations  2.68 us (1%)
    psum x1, blocking collectives, local(): curvature = lax.psum(board, ('seq', 'dp'))  40.5 us
    unnamed x76, local copies, waits for them, and re-layouts  9.05 us
    all_to_all x1, waiting for transfers between devices, local(): lax.all_to_all(to_items(queries), 'seq', split_axis=0, concat_axis=1, til...  9 us
    all_to_all x1, waiting for transfers between devices, local(): lax.all_to_all(to_items(key_rows), 'seq', split_axis=0, concat_axis=1, ti...  9 us
    all_to_all x1, waiting for transfers between devices, local(): lax.all_to_all(to_items(key_tangent), 'seq', split_axis=0, concat_axis=1,...  8.73 us
    dot_general x8, matrix products, inner_rows(): lax.dot_general(left, right, (((1,), (1,)), ((), ())), preferred_element_...  8.68 us
    all_to_all x1, starting transfers between devices, local(): lax.all_to_all(to_items(queries), 'seq', split_axis=0, concat_axis=1, til...  7.39 us
    unnamed x3, other arithmetic  7.33 us
  transfers between devices with their start and end apart: 9, of which 8 were waited for; matrix products, arithmetic and copies ran while one was open for 14% of the time, Pallas kernels for 0%

commit v1 on v0

--- a/solution.py
+++ b/solution.py
@@ -98,7 +98,15 @@
         lax.all_to_all(to_items(key_rows), "seq", split_axis=0, concat_axis=1, tiled=True),
         lax.all_to_all(to_items(value_rows), "seq", split_axis=0, concat_axis=1, tiled=True),
         lax.all_to_all(to_items(query_tangent), "seq", split_axis=0, concat_axis=1, tiled=True),
-        lax.all_to_all(to_items(key_tangent), "seq", split_axis=0, concat_axis=1, tiled=True),
+        jnp.concatenate(
+            lax.all_to_all(
+                jnp.stack(jnp.split(to_items(key_tangent), lax.axis_size("seq"), axis=0)),
+                "seq",
+                0,
+                0,
+            ),
+            axis=1,
+        ),
         lax.all_to_all(to_items(out_adjoint), "seq", split_axis=0, concat_axis=1, tiled=True),
     )
     item_count = parts[0].shape[0]

time: 183 us -> 190 us (1.038)
  local copies, waits for them, and re-layouts: 18.6 us -> 29.8 us
  waiting for transfers between devices: 53.8 us -> 45.7 us
  starting transfers between devices: 36.8 us -> 39.9 us
    unnamed x76 -> x94, local copies, waits for them, and re-layouts: 9.05 us -> 20.4 us
    all_to_all x1, waiting for transfers between devices: 9 us -> 0.01 us  [local(): lax.all_to_all(to_items(queries), 'seq', split_axis=0, concat_axis=1, til...]
    all_to_all x1, starting transfers between devices: 3.53 us -> 6.02 us  [local(): lax.all_to_all(to_items(key_rows), 'seq', split_axis=0, concat_axis=1, ti...]
    transpose x12 -> x10, local copies, waits for them, and re-layouts: 4.64 us -> 3.89 us  [to_items(): jnp.transpose(shaped, (0, 2, 1, 3))]
  transfers between devices with their start and end apart: 9 -> 9, of which waited for: 8 -> 7; matrix products, arithmetic and copies ran while one was open for 14% -> 19% of each run, Pallas kernels for 0% -> 0%
where the time goes in v1:
time: 190 us; the launch traced here: 188 us
  waiting for transfers between devices  45.7 us (24%)
  blocking collectives  40.5 us (21%)
  starting transfers between devices  39.9 us (21%)
  local copies, waits for them, and re-layouts  29.8 us (16%)
  matrix products  17.1 us (9%)
  other arithmetic  12.7 us (7%)
  between operations  2.64 us (1%)
    psum x1, blocking collectives, local(): curvature = lax.psum(board, ('seq', 'dp'))  40.5 us
    unnamed x94, local copies, waits for them, and re-layouts  20.4 us
    all_to_all x1, waiting for transfers between devices, local(): lax.all_to_all(to_items(key_rows), 'seq', split_axis=0, concat_axis=1, ti...  9.06 us
    all_to_all x1, waiting for transfers between devices, local(): lax.all_to_all(jnp.stack(jnp.split(to_items(key_tangent), lax.axis_size('...  8.72 us
    dot_general x8, matrix products, inner_rows(): lax.dot_general(left, right, (((1,), (1,)), ((), ())), preferred_element_...  8.65 us
    unnamed x3, other arithmetic  8.03 us
    all_to_all x1, waiting for transfers between devices, local(): lax.all_to_all(to_items(out_adjoint), 'seq', split_axis=0, concat_axis=1,...  7.54 us
    all_to_all x1, starting transfers between devices, local(): lax.all_to_all(to_items(queries), 'seq', split_axis=0, concat_axis=1, til...  7.39 us
  transfers between devices with their start and end apart: 9, of which 7 were waited for; matrix products, arithmetic and copies ran while one was open for 19% of the time, Pallas kernels for 0%

profile of v1, /device:TPU:0, one launch (start us, length us, event | category | flops | bytes accessed | tf_op | source)
XLA Modules:
  0.0 188.4 jit_solution(10603383341389421545)
XLA Ops:
  2.5 7.4 %all-to-all-start = ((bf16[16,64,128]{2,1,0:T(8,128)(2,1)}), bf16[16,64,128]{2,1,0:T(8,128)(2,1)S(1)}, u32[]{:S(2)}, u32[]{:S(2)}) async-start(bf16[16,64,128]{2,1,0:T(8,128)(2,1)} %bitcast.1), calls=%async_computation | async-start | bytes 524288 | tf_op jit(solution)/shard_map/all_to_all | solution.py:97
  20.1 6.0 %all-to-all-start.1 = ((bf16[16,64,128]{2,1,0:T(8,128)(2,1)}), bf16[16,64,128]{2,1,0:T(8,128)(2,1)S(1)}, u32[]{:S(2)}, u32[]{:S(2)}) async-start(bf16[16,64,128]{2,1,0:T(8,128)(2,1)} %bitcast.4), calls=%async_computation.1 | async-start | bytes 524288 | tf_op jit(solution)/shard_map/all_to_all | solution.py:98
  27.0 9.1 %all-to-all-done.1 = bf16[16,64,128]{2,1,0:T(8,128)(2,1)S(1)} async-done(((bf16[16,64,128]{2,1,0:T(8,128)(2,1)}), bf16[16,64,128]{2,1,0:T(8,128)(2,1)S(1)}, u32[]{:S(2)}, u32[]{:S(2)}) %all-to-all-start.1) | async-done | bytes 262176 | tf_op jit(solution)/shard_map/all_to_all | solution.py:98
  36.1 3.5 %all-to-all-start.2 = ((bf16[16,64,128]{2,1,0:T(8,128)(2,1)}), bf16[16,64,128]{2,1,0:T(8,128)(2,1)S(1)}, u32[]{:S(2)}, u32[]{:S(2)}) async-start(bf16[16,64,128]{2,1,0:T(8,128)(2,1)} %bitcast.7), calls=%async_computation.2 | async-start | bytes 524288 | tf_op jit(solution)/shard_map/all_to_all | solution.py:100
  43.0 6.6 %all-to-all-done.2 = bf16[16,64,128]{2,1,0:T(8,128)(2,1)S(1)} async-done(((bf16[16,64,128]{2,1,0:T(8,128)(2,1)}), bf16[16,64,128]{2,1,0:T(8,128)(2,1)S(1)}, u32[]{:S(2)}, u32[]{:S(2)}) %all-to-all-start.2) | async-done | bytes 262176 | tf_op jit(solution)/shard_map/all_to_all | solution.py:100
  49.6 3.5 %all-to-all-start.4 = ((bf16[16,64,128]{2,1,0:T(8,128)(2,1)}), bf16[16,64,128]{2,1,0:T(8,128)(2,1)S(1)}, u32[]{:S(2)}, u32[]{:S(2)}) async-start(bf16[16,64,128]{2,1,0:T(8,128)(2,1)} %bitcast.31), calls=%async_computation.4 | async-start | bytes 524288 | tf_op jit(solution)/shard_map/all_to_all | solution.py:110
  53.8 1.8 fusion.27
  55.6 7.5 %all-to-all-done.4 = bf16[16,64,128]{2,1,0:T(8,128)(2,1)S(1)} async-done(((bf16[16,64,128]{2,1,0:T(8,128)(2,1)}), bf16[16,64,128]{2,1,0:T(8,128)(2,1)S(1)}, u32[]{:S(2)}, u32[]{:S(2)}) %all-to-all-start.4) | async-done | bytes 262176 | tf_op jit(solution)/shard_map/all_to_all | solution.py:110
  63.1 3.5 %all-to-all-start.3 = ((bf16[16,1,64,128]{3,2,1,0:T(8,128)(2,1)}), bf16[16,1,64,128]{3,2,1,0:T(8,128)(2,1)S(1)}, u32[]{:S(2)}, u32[]{:S(2)}) async-start(bf16[16,1,64,128]{3,2,1,0:T(8,128)(2,1)} %constant_dynamic-update-slice_fusion), calls=%async_computation.3 | async-start | bytes 524288 | tf_op jit(solution)/shard_map/all_to_all | solution.py:102
  67.9 8.7 %all-to-all-done.3 = bf16[16,1,64,128]{3,2,1,0:T(8,128)(2,1)S(1)} async-done(((bf16[16,1,64,128]{3,2,1,0:T(8,128)(2,1)}), bf16[16,1,64,128]{3,2,1,0:T(8,128)(2,1)S(1)}, u32[]{:S(2)}, u32[]{:S(2)}) %all-to-all-start.3) | async-done | bytes 262176 | tf_op jit(solution)/shard_map/all_to_all | solution.py:102
  76.7 3.7 %all-to-all-start.5 = ((bf16[16,64,128]{2,1,0:T(8,128)(2,1)}), bf16[16,64,128]{2,1,0:T(8,128)(2,1)S(1)}, u32[]{:S(2)}, u32[]{:S(2)}) async-start(bf16[16,64,128]{2,1,0:T(8,128)(2,1)} %bitcast.34), calls=%async_computation.5 | async-start | bytes 524288 | tf_op jit(solution)/shard_map/all_to_all | solution.py:99
  82.0 2.1 %multiply_reduce_fusion.2 = (f32[512]{0:T(512)S(1)}, f32[512,1024]{1,0:T(8,128)}) fusion(f32[512]{0:T(512)S(1)} %fusion.2, f32[512,1024]{1,0:T(8,128)S(1)} %get-tuple-element.85, f32[512]{0:T(512)S(1)} %get-tuple-element.84, f32[512,1024]{1,0:T(8,128)S(1)} %copy-done.11, bf16[1024,128]{1,0:T(8,128)(2,1)S(1)} %bitcast.217, bf16[512,128]{1,0:T(8,128)(2,1)S(1)} %bitcast.264), kind=kOutput, calls=%fused_computation.7 | convolution fusion | flops 137362944 | bytes 6690816 | tf_op jit(solution)/shard_map/dot_general | solution.py:10
  84.1 6.1 %all-to-all-done.5 = bf16[16,64,128]{2,1,0:T(8,128)(2,1)S(1)} async-done(((bf16[16,64,128]{2,1,0:T(8,128)(2,1)}), bf16[16,64,128]{2,1,0:T(8,128)(2,1)S(1)}, u32[]{:S(2)}, u32[]{:S(2)}) %all-to-all-start.5) | async-done | bytes 262176 | tf_op jit(solution)/shard_map/all_to_all | solution.py:99
  90.2 2.7 %multiply_reduce_fusion.1 = (f32[512]{0:T(512)S(1)}, f32[512]{0:T(512)S(1)}, f32[512,1024]{1,0:T(8,128)S(1)}) fusion(f32[512]{0:T(512)S(1)} %fusion.2, f32[512,1024]{1,0:T(8,128)S(1)} %get-tuple-element.85, f32[512]{0:T(512)S(1)} %get-tuple-element.84, f32[512,1024]{1,0:T(8,128)} %get-tuple-element.87, f32[512]{0:T(512)S(1)} %get-tuple-element.86, ...), kind=kOutput, calls=%fused_computation.5 | convolution fusion | flops 138411008 | bytes 6694912 | tf_op jit(solution)/shard_map/dot_general | solution.py:10
  92.9 1.2 multiply_convert_fusion
  95.4 1.3 fusion.30
  100.0 1.3 multiply_convert_fusion.1
  102.3 1.2 fusion.11
  104.5 2.9 %reduce.12 = bf16[1024,128]{1,0:T(8,128)(2,1)} reduce(bf16[1024,1,128]{2,1,0:T(2,128)(2,1)S(1)} %bitcast.222, bf16[]{:T(256)} %broadcast.116), dimensions={1}, to_apply=%bitcast.206.reduce_sub_computation | reduce | bytes 524290
  107.4 1.8 reshape.291
  109.2 4.4 %all-to-all-start.8 = ((bf16[16,2,4096]{2,1,0:T(2,128)(2,1)}), bf16[16,2,4096]{2,1,0:T(2,128)(2,1)}, u32[]{:S(2)}, u32[]{:S(2)}) async-start(bf16[16,2,4096]{2,1,0:T(2,128)(2,1)} %reshape.291), calls=%async_computation.8 | async-start | bytes 524288 | tf_op jit(solution)/shard_map/all_to_all | solution.py:123
  113.6 1.2 fusion.10
  114.9 1.2 multiply_reduce_fusion.6
  116.5 2.9 %reduce.13 = bf16[1024,128]{1,0:T(8,128)(2,1)} reduce(bf16[1024,1,128]{2,1,0:T(2,128)(2,1)S(1)} %bitcast.225, bf16[]{:T(256)} %broadcast.116), dimensions={1}, to_apply=%bitcast.207.reduce_sub_computation | reduce | bytes 524290
  119.4 1.7 reshape.289
  121.9 1.5 all-to-all-done.8
  123.4 4.2 %all-to-all-start.7 = ((bf16[16,2,4096]{2,1,0:T(2,128)(2,1)}), bf16[16,2,4096]{2,1,0:T(2,128)(2,1)S(1)}, u32[]{:S(2)}, u32[]{:S(2)}) async-start(bf16[16,2,4096]{2,1,0:T(2,128)(2,1)} %reshape.289), calls=%async_computation.7 | async-start | bytes 524288 | tf_op jit(solution)/shard_map/all_to_all | solution.py:122
  128.5 2.2 %reduce.11 = bf16[1024,128]{1,0:T(8,128)(2,1)S(1)} reduce(bf16[1024,1,128]{2,1,0:T(2,128)(2,1)S(1)} %bitcast.224, bf16[]{:T(256)} %broadcast.116), dimensions={1}, to_apply=%bitcast.208.reduce_sub_computation | reduce | bytes 524290
  131.5 6.2 %all-to-all-done.7 = bf16[16,2,4096]{2,1,0:T(2,128)(2,1)S(1)} async-done(((bf16[16,2,4096]{2,1,0:T(2,128)(2,1)}), bf16[16,2,4096]{2,1,0:T(2,128)(2,1)S(1)}, u32[]{:S(2)}, u32[]{:S(2)}) %all-to-all-start.7) | async-done | bytes 262176 | tf_op jit(solution)/shard_map/all_to_all | solution.py:122
  137.6 3.5 %all-to-all-start.6 = ((bf16[16,2,4096]{2,1,0:T(2,128)(2,1)}), bf16[16,2,4096]{2,1,0:T(2,128)(2,1)S(1)}, u32[]{:S(2)}, u32[]{:S(2)}) async-start(bf16[16,2,4096]{2,1,0:T(2,128)(2,1)} %reshape.287), calls=%async_computation.6 | async-start | bytes 524288 | tf_op jit(solution)/shard_map/all_to_all | solution.py:121
  143.4 40.5 %psum.7 = f32[2,16]{1,0:T(2,128)} all-reduce(f32[2,16]{1,0:T(2,128)S(1)} %and_select_fusion), channel_id=1, replica_groups=mesh['seq'=16,'dp'=2] {'seq','dp'}, use_global_device_ids=true, to_apply=%region_12.13 | all-reduce | flops 32 | bytes 256 | tf_op jit(solution)/shard_map/psum | solution.py:142
  183.9 2.2 %reshape.292 = bf16[1024,1,128]{2,1,0:T(2,128)(2,1)S(1)} reshape(bf16[16,2,4096]{2,1,0:T(2,128)(2,1)} %all-to-all-done.8) | data formatting | bytes 524288
  (137 shorter events, 32.0 us)
Async XLA Ops:
  0.6 9.4 %copy-start = (bf16[2,64,1024]{2,1,0:T(8,128)(2,1)S(1)}, bf16[2,64,1024]{2,1,0:T(8,128)(2,1)}, u32[]{:S(2)}) copy-start(bf16[2,64,1024]{2,1,0:T(8,128)(2,1)} %param.22) | copy-start | bytes 786436
  0.6 9.3 %copy-start.24 = (bf16[2,64,1024]{2,1,0:T(8,128)(2,1)S(1)}, bf16[2,64,1024]{2,1,0:T(8,128)(2,1)}, u32[]{:S(2)}) copy-start(bf16[2,64,1024]{2,1,0:T(8,128)(2,1)} %param.19) | copy-start | bytes 786436
  1.7 17.6 %copy-start.25 = (bf16[2,64,1024]{2,1,0:T(8,128)(2,1)S(1)}, bf16[2,64,1024]{2,1,0:T(8,128)(2,1)}, u32[]{:S(2)}) copy-start(bf16[2,64,1024]{2,1,0:T(8,128)(2,1)} %param.21) | copy-start | bytes 786436
  2.5 17.5 %all-to-all-start = ((bf16[16,64,128]{2,1,0:T(8,128)(2,1)}), bf16[16,64,128]{2,1,0:T(8,128)(2,1)S(1)}, u32[]{:S(2)}, u32[]{:S(2)}) async-start(bf16[16,64,128]{2,1,0:T(8,128)(2,1)} %bitcast.1), calls=%async_computation | async-start | bytes 524288 | tf_op jit(solution)/shard_map/all_to_all | solution.py:97
  9.9 16.2 %copy-start.26 = (bf16[2,64,1024]{2,1,0:T(8,128)(2,1)S(1)}, bf16[2,64,1024]{2,1,0:T(8,128)(2,1)}, u32[]{:S(2)}) copy-start(bf16[2,64,1024]{2,1,0:T(8,128)(2,1)} %param.20) | copy-start | bytes 786436
  10.0 16.9 %copy-start.27 = (bf16[2,64,1024]{2,1,0:T(8,128)(2,1)S(1)}, bf16[2,64,1024]{2,1,0:T(8,128)(2,1)}, u32[]{:S(2)}) copy-start(bf16[2,64,1024]{2,1,0:T(8,128)(2,1)} %param.23) | copy-start | bytes 786436
  20.1 16.0 %all-to-all-start.1 = ((bf16[16,64,128]{2,1,0:T(8,128)(2,1)}), bf16[16,64,128]{2,1,0:T(8,128)(2,1)S(1)}, u32[]{:S(2)}, u32[]{:S(2)}) async-start(bf16[16,64,128]{2,1,0:T(8,128)(2,1)} %bitcast.4), calls=%async_computation.1 | async-start | bytes 524288 | tf_op jit(solution)/shard_map/all_to_all | solution.py:98
  36.1 31.3 %copy-start.4 = (bf16[16,64,128]{2,1,0:T(8,128)(2,1)}, bf16[16,64,128]{2,1,0:T(8,128)(2,1)S(1)}, u32[]{:S(2)}) copy-start(bf16[16,64,128]{2,1,0:T(8,128)(2,1)S(1)} %all-to-all-done.1) | copy-start | bytes 786436
  36.1 13.5 %all-to-all-start.2 = ((bf16[16,64,128]{2,1,0:T(8,128)(2,1)}), bf16[16,64,128]{2,1,0:T(8,128)(2,1)S(1)}, u32[]{:S(2)}, u32[]{:S(2)}) async-start(bf16[16,64,128]{2,1,0:T(8,128)(2,1)} %bitcast.7), calls=%async_computation.2 | async-start | bytes 524288 | tf_op jit(solution)/shard_map/all_to_all | solution.py:100
  49.6 13.5 %copy-start.9 = (bf16[16,64,128]{2,1,0:T(8,128)(2,1)}, bf16[16,64,128]{2,1,0:T(8,128)(2,1)S(1)}, u32[]{:S(2)}) copy-start(bf16[16,64,128]{2,1,0:T(8,128)(2,1)S(1)} %all-to-all-done.2) | copy-start | bytes 786436
  49.6 13.5 %all-to-all-start.4 = ((bf16[16,64,128]{2,1,0:T(8,128)(2,1)}), bf16[16,64,128]{2,1,0:T(8,128)(2,1)S(1)}, u32[]{:S(2)}, u32[]{:S(2)}) async-start(bf16[16,64,128]{2,1,0:T(8,128)(2,1)} %bitcast.31), calls=%async_computation.4 | async-start | bytes 524288 | tf_op jit(solution)/shard_map/all_to_all | solution.py:110
  53.8 13.5 %copy-start.16 = (bf16[8,64,128]{2,1,0:T(8,128)(2,1)}, bf16[8,64,128]{2,1,0:T(8,128)(2,1)S(1)}, u32[]{:S(2)}) copy-start(bf16[8,64,128]{2,1,0:T(8,128)(2,1)S(1)} %get-tuple-element.79) | copy-start | bytes 393220
  63.1 13.5 %all-to-all-start.3 = ((bf16[16,1,64,128]{3,2,1,0:T(8,128)(2,1)}), bf16[16,1,64,128]{3,2,1,0:T(8,128)(2,1)S(1)}, u32[]{:S(2)}, u32[]{:S(2)}) async-start(bf16[16,1,64,128]{3,2,1,0:T(8,128)(2,1)} %constant_dynamic-update-slice_fusion), calls=%async_computation.3 | async-start | bytes 524288 | tf_op jit(solution)/shard_map/all_to_all | solution.py:102
  67.4 22.8 %copy-start.28 = (bf16[8,64,128]{2,1,0:T(8,128)(2,1)}, bf16[8,64,128]{2,1,0:T(8,128)(2,1)S(1)}, u32[]{:S(2)}) copy-start(bf16[8,64,128]{2,1,0:T(8,128)(2,1)S(1)} %get-tuple-element.83) | copy-start | bytes 393220
  76.7 7.4 %copy-start.6 = (bf16[16,1,64,128]{3,2,1,0:T(8,128)(2,1)}, bf16[16,1,64,128]{3,2,1,0:T(8,128)(2,1)S(1)}, u32[]{:S(2)}) copy-start(bf16[16,1,64,128]{3,2,1,0:T(8,128)(2,1)S(1)} %all-to-all-done.3) | copy-start | bytes 786436
  76.7 13.5 %all-to-all-start.5 = ((bf16[16,64,128]{2,1,0:T(8,128)(2,1)}), bf16[16,64,128]{2,1,0:T(8,128)(2,1)S(1)}, u32[]{:S(2)}, u32[]{:S(2)}) async-start(bf16[16,64,128]{2,1,0:T(8,128)(2,1)} %bitcast.34), calls=%async_computation.5 | async-start | bytes 524288 | tf_op jit(solution)/shard_map/all_to_all | solution.py:99
  90.2 2.7 %copy-start.19 = (bf16[16,64,128]{2,1,0:T(8,128)(2,1)}, bf16[16,64,128]{2,1,0:T(8,128)(2,1)S(1)}, u32[]{:S(2)}) copy-start(bf16[16,64,128]{2,1,0:T(8,128)(2,1)S(1)} %all-to-all-done.5) | copy-start | bytes 786436
  90.2 2.7 %copy-start.13 = (f32[512,1024]{1,0:T(8,128)S(1)}, f32[512,1024]{1,0:T(8,128)}, u32[]{:S(2)}) copy-start(f32[512,1024]{1,0:T(8,128)} %get-tuple-element.87) | copy-start | bytes 6291460
  94.2 2.8 %copy-start.23 = (bf16[8,64,128]{2,1,0:T(8,128)(2,1)S(1)}, bf16[8,64,128]{2,1,0:T(8,128)(2,1)}, u32[]{:S(2)}) copy-start(bf16[8,64,128]{2,1,0:T(8,128)(2,1)} %get-tuple-element.80) | copy-start | bytes 393220
  103.5 10.1 %copy-start.3 = (bf16[512,512]{0,1:T(8,128)(2,1)S(1)}, bf16[512,512]{0,1:T(8,128)(2,1)}, u32[]{:S(2)}) copy-start(bf16[512,512]{0,1:T(8,128)(2,1)} %get-tuple-element.74) | copy-start | bytes 1572868
  103.5 10.1 %copy-start.15 = (bf16[8,64,128]{2,1,0:T(8,128)(2,1)S(1)}, bf16[8,64,128]{2,1,0:T(8,128)(2,1)}, u32[]{:S(2)}) copy-start(bf16[8,64,128]{2,1,0:T(8,128)(2,1)} %get-tuple-element.78) | copy-start | bytes 393220
  103.5 11.3 %copy-start.8 = (bf16[16,1,64,128]{3,2,1,0:T(8,128)(2,1)S(1)}, bf16[16,1,64,128]{3,2,1,0:T(8,128)(2,1)}, u32[]{:S(2)}) copy-start(bf16[16,1,64,128]{3,2,1,0:T(8,128)(2,1)} %copy-done.6) | copy-start | bytes 786436
  103.6 11.3 %copy-start.12 = (f32[1024,128]{1,0:T(8,128)S(1)}, f32[1024,128]{1,0:T(8,128)}, u32[]{:S(2)}) copy-start(f32[1024,128]{1,0:T(8,128)} %fusion.30) | copy-start | bytes 1572868
  103.6 11.3 %copy-start.17 = (bf16[8,64,128]{2,1,0:T(8,128)(2,1)S(1)}, bf16[8,64,128]{2,1,0:T(8,128)(2,1)}, u32[]{:S(2)}) copy-start(bf16[8,64,128]{2,1,0:T(8,128)(2,1)} %copy-done.16) | copy-start | bytes 393220
  109.2 14.2 %all-to-all-start.8 = ((bf16[16,2,4096]{2,1,0:T(2,128)(2,1)}), bf16[16,2,4096]{2,1,0:T(2,128)(2,1)}, u32[]{:S(2)}, u32[]{:S(2)}) async-start(bf16[16,2,4096]{2,1,0:T(2,128)(2,1)} %reshape.291), calls=%async_computation.8 | async-start | bytes 524288 | tf_op jit(solution)/shard_map/all_to_all | solution.py:123
  114.9 6.2 %copy-start.2 = (bf16[512,512]{0,1:T(8,128)(2,1)S(1)}, bf16[512,512]{0,1:T(8,128)(2,1)}, u32[]{:S(2)}) copy-start(bf16[512,512]{0,1:T(8,128)(2,1)} %copy-done.1) | copy-start | bytes 1572868
  116.1 5.4 %copy-start.18 = (f32[512,128]{1,0:T(8,128)S(1)}, f32[512,128]{1,0:T(8,128)}, u32[]{:S(2)}) copy-start(f32[512,128]{1,0:T(8,128)} %fusion.28) | copy-start | bytes 786436
  121.5 6.2 %copy-start.22 = (bf16[8,1,64,128]{3,2,1,0:T(8,128)(2,1)S(1)}, bf16[8,1,64,128]{3,2,1,0:T(8,128)(2,1)}, u32[]{:S(2)}) copy-start(bf16[8,1,64,128]{3,2,1,0:T(8,128)(2,1)} %copy-done.21) | copy-start | bytes 393220
  123.4 14.2 %all-to-all-start.7 = ((bf16[16,2,4096]{2,1,0:T(2,128)(2,1)}), bf16[16,2,4096]{2,1,0:T(2,128)(2,1)S(1)}, u32[]{:S(2)}, u32[]{:S(2)}) async-start(bf16[16,2,4096]{2,1,0:T(2,128)(2,1)} %reshape.289), calls=%async_computation.7 | async-start | bytes 524288 | tf_op jit(solution)/shard_map/all_to_all | solution.py:122
  128.0 13.2 %copy-start.10 = (bf16[16,64,128]{2,1,0:T(8,128)(2,1)S(1)}, bf16[16,64,128]{2,1,0:T(8,128)(2,1)}, u32[]{:S(2)}) copy-start(bf16[16,64,128]{2,1,0:T(8,128)(2,1)} %copy-done.9) | copy-start | bytes 786436
  128.1 15.2 %copy-start.31 = (pred[16]{0:T(512)(128)(4,1)S(1)}, pred[16]{0:T(512)(128)(4,1)}, u32[]{:S(2)}) copy-start(pred[16]{0:T(512)(128)(4,1)} %iota_compare_fusion.2) | copy-start | bytes 52
  137.6 48.8 %all-to-all-start.6 = ((bf16[16,2,4096]{2,1,0:T(2,128)(2,1)}), bf16[16,2,4096]{2,1,0:T(2,128)(2,1)S(1)}, u32[]{:S(2)}, u32[]{:S(2)}) async-start(bf16[16,2,4096]{2,1,0:T(2,128)(2,1)} %reshape.287), calls=%async_computation.6 | async-start | bytes 524288 | tf_op jit(solution)/shard_map/all_to_all | solution.py:121
  (9 other events, 13.4 us)
